TPU v7x, 32 devices: a whole 2x2x4 slice. The times are simulated.
32 devices in a mesh: frame: 4 (over y, x), sector: 8 (over z, core).
Axes of the slice: x: 2, y: 2, z: 4, core: 2. Of those that a mesh axis runs over, the one named last changes fastest.
Arguments:
- camera: bfloat16 [4096, 1536], P(('frame', 'sector')), may hold values from -6 to 6
- owners: int32 [256], P(('frame', 'sector')), may hold values from 0 to 7, as said below
- unit_slots: int32 [256, 8], P(('frame', 'sector')), may hold values from 0 to 15, as said below
- pool_weights: bfloat16 [256, 8, 16, 128], P(('frame', 'sector')), may hold values from -0.0234375 to 0.0234375
- student: bfloat16 [32768, 512], P(('frame', 'sector')), may hold values from -0.25 to 0.25
- head_weight: bfloat16 [1536, 512], replicated, may hold values from -0.15625 to 0.15625
Outputs:
- grad_student: bfloat16 [32768, 512], P(('frame', 'sector'))
- grad_head: float32 [1536, 512], P('sector')
Inputs may be any that keep to these rules, and one draw needn't show every extreme that they name: `owners`: in every frame group a device sends at most 2 of its units to any one sector, one sector receives exactly 2 units from every device of the group, and every sector receives at least one unit. `unit_slots`: an entry q of a lidar block held by sector o of frame group f names the unit of rank q % 2 among the units of device q // 2 of group f that are owned by o; that unit exists, and every unit is named by at least one entry of its owner.
All inputs are finite; a program needn't handle non-finite values.
Results may differ from a plain program's by a relative error of at most 0.005.
Values may be sent and summed in bfloat16 or wider, within the bound.
A program may use at most 64 MiB of HBM per device.

v0:
```python
import jax
import jax.numpy as jnp
from jax import lax
from jax.sharding import PartitionSpec as P

CAP = 2
LOSS_WEIGHT = 8.0
EPSILON = 1e-06


def cosine_grads(target, student):
    learner = student.astype(jnp.float32)
    norm_teacher = jnp.sqrt(jnp.sum(target * target, axis=-1, keepdims=True) + EPSILON)
    norm_learner = jnp.sqrt(jnp.sum(learner * learner, axis=-1, keepdims=True) + EPSILON)
    cosine = jnp.sum(target * learner, axis=-1, keepdims=True) / (norm_teacher * norm_learner)
    grad_learner = -LOSS_WEIGHT * (
        target / (norm_teacher * norm_learner) - cosine * learner / (norm_learner * norm_learner)
    )
    grad_teacher = -LOSS_WEIGHT * (
        learner / (norm_teacher * norm_learner) - cosine * target / (norm_teacher * norm_teacher)
    )
    return (grad_teacher.astype(jnp.bfloat16), grad_learner.astype(jnp.bfloat16))


def project_rows(features, head_weight):
    return jnp.dot(features, head_weight, preferred_element_type=jnp.float32).astype(jnp.bfloat16)


def on_device(camera, owners, unit_slots, pool_weights, student, head_weight):
    sectors = lax.axis_size("sector")
    count_units = owners.shape[0]
    unit_rows = camera.shape[0] // count_units
    width = camera.shape[1]
    head_width = head_weight.shape[1]
    blocks, per_block = unit_slots.shape
    block_rows = pool_weights.shape[3]
    earlier = jnp.arange(count_units)[:, None] > jnp.arange(count_units)[None, :]
    matching = owners[:, None] == owners[None, :]
    rank_of = jnp.sum(jnp.where(earlier & matching, 1, 0), axis=1).astype(jnp.int32)
    destination = owners * CAP + rank_of
    placing = (jnp.arange(sectors * CAP)[:, None] == destination[None, :]).astype(jnp.bfloat16)
    flat_slots = unit_slots.reshape(-1)
    packed = jnp.dot(
        placing, camera.reshape(count_units, unit_rows * width), preferred_element_type=jnp.float32
    ).astype(jnp.bfloat16)
    packed = packed.reshape(sectors, CAP, unit_rows, width)
    arrived = lax.all_to_all(packed, "sector", split_axis=0, concat_axis=0, tiled=True).reshape(
        sectors * CAP * unit_rows, width
    )
    slot_proj = project_rows(arrived, head_weight).reshape(sectors * CAP, unit_rows, head_width)
    chosen = jnp.take(slot_proj, flat_slots, axis=0).reshape(
        blocks, per_block, unit_rows, head_width
    )
    target = jnp.einsum(
        "bkjl,bkjh->blh", pool_weights, chosen, preferred_element_type=jnp.float32
    ).reshape(blocks * block_rows, head_width)
    grad_teacher, grad_student = cosine_grads(target, student)
    spread = jnp.einsum(
        "bkjl,blh->bkjh",
        pool_weights,
        grad_teacher.reshape(blocks, block_rows, head_width),
        preferred_element_type=jnp.float32,
    )
    slot_grad = jax.ops.segment_sum(
        spread.reshape(blocks * per_block, unit_rows * head_width),
        flat_slots,
        num_segments=sectors * CAP,
    ).astype(jnp.bfloat16)
    row_grads = slot_grad.reshape(sectors * CAP * unit_rows, head_width)
    sector_sums = lax.psum_scatter(
        lax.dot_general(
            arrived, row_grads, (((0,), (0,)), ((), ())), preferred_element_type=jnp.float32
        ),
        "sector",
        scatter_dimension=0,
        tiled=True,
    )
    grad_head = lax.psum(sector_sums, "frame")
    return (grad_student, grad_head)


def solution(mesh):
    return jax.shard_map(
        on_device,
        mesh=mesh,
        in_specs=(
            P(("frame", "sector"), None),
            P(("frame", "sector")),
            P(("frame", "sector"), None),
            P(("frame", "sector"), None, None, None),
            P(("frame", "sector"), None),
            P(),
        ),
        out_specs=(P(("frame", "sector"), None), P("sector", None)),
        check_vma=False,
    )
```

profile of v0, /device:TPU:0, one launch (start us, length us, event | category | flops | bytes accessed | tf_op | source)
XLA Modules:
  0.0 148.0 jit_solution(6833077229085780709)
XLA Ops:
  7.2 0.0 copy-start
  7.2 1.3 reshape.112
  8.5 0.9 select_reduce_fusion
  9.4 0.7 multiply_add_fusion
  10.1 0.0 copy-start.5
  10.1 0.3 convolution_convert_fusion
  10.4 1.1 copy.10
  11.5 6.3 %all-to-all-start = ((bf16[8,2,16,1536]{3,2,1,0:T(8,128)(2,1)}), bf16[8,2,16,1536]{3,2,1,0:T(8,128)(2,1)S(1)}, u32[]{:S(2)}, u32[]{:S(2)}) async-start(bf16[8,2,16,1536]{3,2,1,0:T(8,128)(2,1)} %bitcast.19), calls=%async_computation | async-start | bytes 1572864 | tf_op jit(solution)/shard_map/all_to_all | solution.py:47
  17.9 0.0 reduce-scatter.2.cloned.1.call-start
  17.9 0.0 copy-done.5
  17.9 0.1 reshape.116
  18.0 0.1 reshape.131
  18.1 20.7 %all-to-all-done = bf16[8,2,16,1536]{3,2,1,0:T(8,128)(2,1)S(1)} async-done(((bf16[8,2,16,1536]{3,2,1,0:T(8,128)(2,1)}), bf16[8,2,16,1536]{3,2,1,0:T(8,128)(2,1)S(1)}, u32[]{:S(2)}, u32[]{:S(2)}) %all-to-all-start) | async-done | bytes 786464 | tf_op jit(solution)/shard_map/all_to_all | solution.py:47
  38.8 0.0 copy-start.2
  38.8 0.0 copy-done
  38.8 0.0 copy-start.4
  38.8 0.6 convolution_convert_fusion.1
  39.4 0.3 copy-done.2
  39.7 0.6 gather_fusion
  40.4 0.0 copy-start.1
  40.4 0.0 copy-done.4
  40.4 0.6 fusion.9
  41.0 0.6 copy-done.1
  41.6 0.4 fusion.1
  42.0 2.2 %fusion.7 = (bf16[1024,512]{1,0:T(8,128)(2,1)S(1)}, bf16[1024,512]{1,0:T(8,128)(2,1)}) fusion(bf16[1024,512]{1,0:T(8,128)(2,1)S(1)} %copy-done.1, f32[8,512,128,1]{1,2,3,0:T(8,128)S(1)} %get-tuple-element.11, f32[1024]{0:T(1024)S(1)} %get-tuple-element.8, f32[1024]{0:T(1024)S(1)} %get-tuple-element.4, f32[1024]{0:T(1024)S(1)} %get-tuple-element.5, ...), kind=kLoop, calls=%fused_computation.14 | loop fusion | flops 6815744 | bytes 5259264 | tf_op jit(solution)/shard_map/convert_element_type | solution.py:22
  44.2 0.4 convolution_bitcast_fusion
  44.6 0.0 copy-start.3
  44.6 2.5 %copy.11 = f32[8,8,16,512]{3,1,2,0:T(8,128)} copy(f32[8,8,16,512]{3,2,1,0:T(8,128)S(1)} %convolution_bitcast_fusion) | data formatting | bytes 4194304
  47.2 4.2 %scatter_custom_fusion = f32[16,8192]{1,0:T(8,128)S(1)} fusion(s32[64]{0:T(128)S(1)} %reshape.131, f32[64,8192]{1,0:T(8,128)} %bitcast.55, f32[]{:T(128)} %constant.8.clone.1), kind=kCustom, calls=%fused_computation.27 | custom fusion | flops 524288 | bytes 524800 | tf_op jit(solution)/shard_map/scatter-add | solution.py:64
  51.4 0.1 reshape.120
  51.5 0.0 copy-done.3
  51.5 2.3 %fusion.23 = f32[1536,512]{1,0:T(8,128)} fusion(bf16[256,1536]{1,0:T(8,128)(2,1)S(1)} %bitcast.53, bf16[256,512]{1,0:T(8,128)(2,1)S(1)} %reshape.120), kind=kOutput, calls=%fused_computation.47 | convolution fusion | flops 402653184 | bytes 4194304 | tf_op jit(solution)/shard_map/dot_general | solution.py:71
  53.8 0.0 reduce-scatter.2.cloned.1.call-update
  53.8 0.0 all-reduce.2.cloned.1.call-start
  53.9 39.4 %reduce-scatter.2.cloned.1.call-done = f32[192,512]{1,0:T(8,128)} async-done(((f32[1536,512]{1,0:T(8,128)}), f32[192,512]{1,0:T(8,128)}) %reduce-scatter.2.cloned.1.call-update) | async-done | bytes 393232 | tf_op jit(solution)/shard_map/reduce_scatter | solution.py:70
  93.2 0.0 all-reduce.2.cloned.1.call-update
  93.2 46.1 %all-reduce.2.cloned.1.call-done = f32[192,512]{1,0:T(8,128)} async-done(((f32[192,512]{1,0:T(8,128)}), f32[192,512]{1,0:T(8,128)}) %all-reduce.2.cloned.1.call-update) | async-done | bytes 393232 | tf_op jit(solution)/shard_map/psum | solution.py:78
  139.4 1.8 %copy.13 = f32[192,512]{1,0:T(8,128)} copy(f32[192,512]{1,0:T(8,128)} %all-reduce.2.cloned.1.call-done) | data formatting | bytes 786432
  (5 shorter events, 0.1 us)
Async XLA Ops:
  7.2 31.7 %copy-start = (bf16[1536,512]{1,0:T(8,128)(2,1)S(1)}, bf16[1536,512]{1,0:T(8,128)(2,1)}, u32[]{:S(2)}) copy-start(bf16[1536,512]{1,0:T(8,128)(2,1)} %param.11) | copy-start | bytes 4718596
  10.1 7.8 %copy-start.5 = (s32[8,8]{1,0:T(8,128)S(1)}, s32[8,8]{1,0:T(8,128)}, u32[]{:S(2)}) copy-start(s32[8,8]{1,0:T(8,128)} %param.8) | copy-start | bytes 772
  11.5 27.3 %all-to-all-start = ((bf16[8,2,16,1536]{3,2,1,0:T(8,128)(2,1)}), bf16[8,2,16,1536]{3,2,1,0:T(8,128)(2,1)S(1)}, u32[]{:S(2)}, u32[]{:S(2)}) async-start(bf16[8,2,16,1536]{3,2,1,0:T(8,128)(2,1)} %bitcast.19), calls=%async_computation | async-start | bytes 1572864 | tf_op jit(solution)/shard_map/all_to_all | solution.py:47
  17.9 75.4 %reduce-scatter.2.cloned.1.call-start = ((), (), s32[]{:S(2)}) async-start(), calls=%async_computation.2 | async-start | bytes 3538944 | tf_op jit(solution)/shard_map/reduce_scatter | solution.py:70
  38.8 0.9 copy-start.2
  38.8 1.5 %copy-start.4 = (bf16[8,8,16,128]{3,2,1,0:T(8,128)(2,1)S(1)}, bf16[8,8,16,128]{3,2,1,0:T(8,128)(2,1)}, u32[]{:S(2)}) copy-start(bf16[8,8,16,128]{3,2,1,0:T(8,128)(2,1)} %param.9) | copy-start | bytes 786436
  40.4 1.2 copy-start.1
  44.6 6.9 %copy-start.3 = (bf16[8,2,16,1536]{3,2,1,0:T(8,128)(2,1)S(1)}, bf16[8,2,16,1536]{3,2,1,0:T(8,128)(2,1)}, u32[]{:S(2)}) copy-start(bf16[8,2,16,1536]{3,2,1,0:T(8,128)(2,1)} %copy-done.2) | copy-start | bytes 2359300
  53.8 85.6 %all-reduce.2.cloned.1.call-start = ((), (), s32[]{:S(2)}) async-start(), calls=%async_computation.3 | async-start | bytes 786432 | tf_op jit(solution)/shard_map/psum | solution.py:78
Sparse Core Ops, SparseCore 0:
  53.9 39.2 reduce-scatter.1
  96.2 43.1 all-reduce.1
where the time goes:
time: 148 us
  waiting for transfers between devices  106 us (72%)
  between operations  14.2 us (10%)
  local copies, waits for them, and re-layouts  8.6 us (6%)
  other arithmetic  8.37 us (6%)
  starting transfers between devices  6.41 us (4%)
  matrix products  4.19 us (3%)
    psum x1, waiting for transfers between devices, on_device(): grad_head = lax.psum(sector_sums, 'frame')  46.1 us
    reduce_scatter x1, waiting for transfers between devices, on_device(): lax.psum_scatter(lax.dot_general(arrived, row_grads, (((0,), (0,)), ((),...  39.4 us
    all_to_all x1, waiting for transfers between devices, on_device(): lax.all_to_all(packed, 'sector', split_axis=0, concat_axis=0, tiled=True)  20.7 us
    unnamed x15, local copies, waits for them, and re-layouts  6.41 us
    all_to_all x1, starting transfers between devices, on_device(): lax.all_to_all(packed, 'sector', split_axis=0, concat_axis=0, tiled=True)  6.33 us
    scatter-add x1, other arithmetic, on_device(): jax.ops.segment_sum(spread.reshape(blocks * per_block, unit_rows * head_w...  4.17 us
  transfers between devices with their start and end apart: 3, of which 3 were waited for; matrix products, arithmetic and copies ran while one was open for 0% of the time, Pallas kernels for 0%

commit v1 on v0

--- a/solution.py
+++ b/solution.py
@@ -1,3 +1,4 @@
+import functools
 import jax
 import jax.numpy as jnp
 from jax import lax
@@ -6,6 +7,13 @@
 CAP = 2
 LOSS_WEIGHT = 8.0
 EPSILON = 1e-06
+
+
+def _shape_surface(w_in, axis_key):
+    return jax.lax.all_gather(w_in, axis_name=axis_key).sum(axis=0)
+
+
+render_ends = functools.partial(_shape_surface, axis_key="frame")
 
 
 def cosine_grads(target, student):
@@ -75,7 +83,7 @@
         scatter_dimension=0,
         tiled=True,
     )
-    grad_head = lax.psum(sector_sums, "frame")
+    grad_head = render_ends(sector_sums)
     return (grad_student, grad_head)
 
 

time: 148 us -> 135 us (0.912)
  waiting for transfers between devices: 106 us -> 92 us
  other arithmetic: 8.37 us -> 10.7 us
  local copies, waits for them, and re-layouts: 8.6 us -> 6.83 us
    psum x1 -> x0, waiting for transfers between devices: 46.1 us -> none  [on_device(): grad_head = lax.psum(sector_sums, 'frame')]
    all_gather x0 -> x1, waiting for transfers between devices: none -> 31.9 us  [_shape_surface(): return jax.lax.all_gather(w_in, axis_name=axis_key).sum(axis=0)]
    reduce_sum x0 -> x1, other arithmetic: none -> 2.34 us  [_shape_surface(): return jax.lax.all_gather(w_in, axis_name=axis_key).sum(axis=0)]
    unnamed x15 -> x14, local copies, waits for them, and re-layouts: 6.41 us -> 4.64 us
where the time goes in v1:
time: 135 us; the launch traced here: 134 us
  waiting for transfers between devices  92 us (68%)
  between operations  14.2 us (11%)
  other arithmetic  10.7 us (8%)
  local copies, waits for them, and re-layouts  6.83 us (5%)
  starting transfers between devices  6.41 us (5%)
  matrix products  4.19 us (3%)
    reduce_scatter x1, waiting for transfers between devices, on_device(): lax.psum_scatter(lax.dot_general(arrived, row_grads, (((0,), (0,)), ((),...  39.4 us
    all_gather x1, waiting for transfers between devices, _shape_surface(): return jax.lax.all_gather(w_in, axis_name=axis_key).sum(axis=0)  31.9 us
    all_to_all x1, waiting for transfers between devices, on_device(): lax.all_to_all(packed, 'sector', split_axis=0, concat_axis=0, tiled=True)  20.7 us
    all_to_all x1, starting transfers between devices, on_device(): lax.all_to_all(packed, 'sector', split_axis=0, concat_axis=0, tiled=True)  6.33 us
    unnamed x14, local copies, waits for them, and re-layouts  4.64 us
    scatter-add x1, other arithmetic, on_device(): jax.ops.segment_sum(spread.reshape(blocks * per_block, unit_rows * head_w...  4.17 us
  transfers between devices with their start and end apart: 3, of which 3 were waited for; matrix products, arithmetic and copies ran while one was open for 0% of the time, Pallas kernels for 0%

profile of v1, /device:TPU:0, one launch (start us, length us, event | category | flops | bytes accessed | tf_op | source)
XLA Modules:
  0.0 134.3 jit_solution(17937041395037864326)
XLA Ops:
  7.2 0.0 copy-start
  7.2 1.3 reshape.112
  8.5 0.9 select_reduce_fusion
  9.4 0.7 multiply_add_fusion
  10.1 0.0 copy-start.5
  10.1 0.3 convolution_convert_fusion
  10.4 1.1 copy.10
  11.5 6.3 %all-to-all-start = ((bf16[8,2,16,1536]{3,2,1,0:T(8,128)(2,1)}), bf16[8,2,16,1536]{3,2,1,0:T(8,128)(2,1)S(1)}, u32[]{:S(2)}, u32[]{:S(2)}) async-start(bf16[8,2,16,1536]{3,2,1,0:T(8,128)(2,1)} %bitcast.20), calls=%async_computation | async-start | bytes 1572864 | tf_op jit(solution)/shard_map/all_to_all | solution.py:55
  17.8 0.0 reduce-scatter.2.cloned.1.call-start
  17.9 0.0 copy-done.5
  17.9 0.1 reshape.116
  18.0 0.1 reshape.131
  18.1 20.7 %all-to-all-done = bf16[8,2,16,1536]{3,2,1,0:T(8,128)(2,1)S(1)} async-done(((bf16[8,2,16,1536]{3,2,1,0:T(8,128)(2,1)}), bf16[8,2,16,1536]{3,2,1,0:T(8,128)(2,1)S(1)}, u32[]{:S(2)}, u32[]{:S(2)}) %all-to-all-start) | async-done | bytes 786464 | tf_op jit(solution)/shard_map/all_to_all | solution.py:55
  38.8 0.0 copy-start.2
  38.8 0.0 copy-done
  38.8 0.0 copy-start.4
  38.8 0.6 convolution_convert_fusion.1
  39.4 0.3 copy-done.2
  39.7 0.6 gather_fusion
  40.4 0.0 copy-start.1
  40.4 0.0 copy-done.4
  40.4 0.6 fusion.9
  41.0 0.6 copy-done.1
  41.6 0.4 fusion.1
  42.0 2.2 %fusion.7 = (bf16[1024,512]{1,0:T(8,128)(2,1)S(1)}, bf16[1024,512]{1,0:T(8,128)(2,1)}) fusion(bf16[1024,512]{1,0:T(8,128)(2,1)S(1)} %copy-done.1, f32[8,512,128,1]{1,2,3,0:T(8,128)S(1)} %get-tuple-element.11, f32[1024]{0:T(1024)S(1)} %get-tuple-element.8, f32[1024]{0:T(1024)S(1)} %get-tuple-element.4, f32[1024]{0:T(1024)S(1)} %get-tuple-element.5, ...), kind=kLoop, calls=%fused_computation.14 | loop fusion | flops 6815744 | bytes 5259264 | tf_op jit(solution)/shard_map/convert_element_type | solution.py:30
  44.2 0.4 convolution_bitcast_fusion
  44.6 0.0 copy-start.3
  44.6 2.5 %copy.11 = f32[8,8,16,512]{3,1,2,0:T(8,128)} copy(f32[8,8,16,512]{3,2,1,0:T(8,128)S(1)} %convolution_bitcast_fusion) | data formatting | bytes 4194304
  47.2 4.2 %scatter_custom_fusion = f32[16,8192]{1,0:T(8,128)S(1)} fusion(s32[64]{0:T(128)S(1)} %reshape.131, f32[64,8192]{1,0:T(8,128)} %bitcast.56, f32[]{:T(128)} %constant.8.clone.1), kind=kCustom, calls=%fused_computation.27 | custom fusion | flops 524288 | bytes 524800 | tf_op jit(solution)/shard_map/scatter-add | solution.py:72
  51.4 0.1 reshape.120
  51.5 0.0 copy-done.3
  51.5 2.3 %fusion.23 = f32[1536,512]{1,0:T(8,128)} fusion(bf16[256,1536]{1,0:T(8,128)(2,1)S(1)} %bitcast.54, bf16[256,512]{1,0:T(8,128)(2,1)S(1)} %reshape.120), kind=kOutput, calls=%fused_computation.47 | convolution fusion | flops 402653184 | bytes 4194304 | tf_op jit(solution)/shard_map/dot_general | solution.py:79
  53.8 0.0 reduce-scatter.2.cloned.1.call-update
  53.8 0.0 all-gather.3.cloned.1.call-start
  53.9 39.4 %reduce-scatter.2.cloned.1.call-done = f32[192,512]{1,0:T(8,128)} async-done(((f32[1536,512]{1,0:T(8,128)}), f32[192,512]{1,0:T(8,128)}) %reduce-scatter.2.cloned.1.call-update) | async-done | bytes 393232 | tf_op jit(solution)/shard_map/reduce_scatter | solution.py:78
  93.2 0.0 all-gather.3.cloned.1.call-update
  93.2 31.9 %all-gather.3.cloned.1.call-done = f32[768,512]{1,0:T(8,128)} async-done(((f32[192,512]{1,0:T(8,128)}), f32[768,512]{1,0:T(8,128)}) %all-gather.3.cloned.1.call-update) | async-done | bytes 1572880 | tf_op jit(solution)/shard_map/all_gather | solution.py:13
  125.2 2.3 %reduce_sum.49 = f32[192,512]{1,0:T(8,128)} reduce(f32[4,192,512]{2,1,0:T(8,128)} %bitcast.57, f32[]{:T(128)} %constant.8.clone.1), dimensions={0}, to_apply=%region_6.7 | reduce | flops 294912 | bytes 1966084 | tf_op jit(solution)/shard_map/reduce_sum | solution.py:13
  (5 shorter events, 0.1 us)
Async XLA Ops:
  7.2 31.7 %copy-start = (bf16[1536,512]{1,0:T(8,128)(2,1)S(1)}, bf16[1536,512]{1,0:T(8,128)(2,1)}, u32[]{:S(2)}) copy-start(bf16[1536,512]{1,0:T(8,128)(2,1)} %param.11) | copy-start | bytes 4718596
  10.1 7.8 %copy-start.5 = (s32[8,8]{1,0:T(8,128)S(1)}, s32[8,8]{1,0:T(8,128)}, u32[]{:S(2)}) copy-start(s32[8,8]{1,0:T(8,128)} %param.8) | copy-start | bytes 772
  11.5 27.3 %all-to-all-start = ((bf16[8,2,16,1536]{3,2,1,0:T(8,128)(2,1)}), bf16[8,2,16,1536]{3,2,1,0:T(8,128)(2,1)S(1)}, u32[]{:S(2)}, u32[]{:S(2)}) async-start(bf16[8,2,16,1536]{3,2,1,0:T(8,128)(2,1)} %bitcast.20), calls=%async_computation | async-start | bytes 1572864 | tf_op jit(solution)/shard_map/all_to_all | solution.py:55
  17.8 75.4 %reduce-scatter.2.cloned.1.call-start = ((), (), s32[]{:S(2)}) async-start(), calls=%async_computation.2 | async-start | bytes 3538944 | tf_op jit(solution)/shard_map/reduce_scatter | solution.py:78
  38.8 0.9 copy-start.2
  38.8 1.5 %copy-start.4 = (bf16[8,8,16,128]{3,2,1,0:T(8,128)(2,1)S(1)}, bf16[8,8,16,128]{3,2,1,0:T(8,128)(2,1)}, u32[]{:S(2)}) copy-start(bf16[8,8,16,128]{3,2,1,0:T(8,128)(2,1)} %param.9) | copy-start | bytes 786436
  40.4 1.2 copy-start.1
  44.6 6.9 %copy-start.3 = (bf16[8,2,16,1536]{3,2,1,0:T(8,128)(2,1)S(1)}, bf16[8,2,16,1536]{3,2,1,0:T(8,128)(2,1)}, u32[]{:S(2)}) copy-start(bf16[8,2,16,1536]{3,2,1,0:T(8,128)(2,1)} %copy-done.2) | copy-start | bytes 2359300
  53.8 71.3 %all-gather.3.cloned.1.call-start = ((), (), s32[]{:S(2)}) async-start(), calls=%async_computation.3 | async-start | bytes 1966080 | tf_op jit(solution)/shard_map/all_gather | solution.py:13
Sparse Core Ops, SparseCore 0:
  53.9 39.2 reduce-scatter.1
  95.1 30.0 all-gather.2
